TPU v7x, 32 devices: a whole 2x2x4 slice. The times are simulated.
32 devices in a mesh: cfg: 2 (over core), seq: 8 (over z, y), mlp: 2 (over x).
Axes of the slice: x: 2, y: 2, z: 4, core: 2. Of those that a mesh axis runs over, the one named last changes fastest.
Arguments:
- image_hidden: bfloat16 [2, 256, 8, 1536], P('cfg', ('seq', 'mlp')), may hold values from -6 to 6
- text_hidden: bfloat16 [2, 1232, 1536], P('cfg', 'seq'), may hold values from -6 to 6
- modulation: float32 [2, 8, 10, 1536], P('cfg'), may hold values from -3 to 3
- text_lengths: int32 [2, 8], P('cfg'), may hold values from 1 to 154, as said below
- timestep: int32 [1], replicated, may hold values from 0 to 27
- latent: float32 [256, 8, 64], P(('seq', 'mlp'), 'cfg'), may hold values from -6 to 6
- w_qkv: bfloat16 [3, 1536, 1536], P(None, None, 'mlp'), may hold values from -0.15625 to 0.15625
- w_out: bfloat16 [1536, 1536], P('mlp'), may hold values from -0.15625 to 0.15625
- w_text_kv: bfloat16 [2, 1536, 1536], P(None, None, 'mlp'), may hold values from -0.15625 to 0.15625
- norm_gain: float32 [3, 64], replicated, may hold values from 1 to 2
- w_up: bfloat16 [1536, 6144], P(None, 'mlp'), may hold values from -0.15625 to 0.15625
- w_down: bfloat16 [6144, 1536], P('mlp'), may hold values from -0.078125 to 0.078125
- w_head: bfloat16 [1536, 64], replicated, may hold values from -0.078125 to 0.078125
Outputs:
- velocity: float32 [256, 8, 64], P(('seq', 'mlp'), 'cfg')
- next_latent: float32 [256, 8, 64], P(('seq', 'mlp'), 'cfg')
- denoised: float32 [256, 8, 64], P(('seq', 'mlp'), 'cfg')
Inputs may be any that keep to these rules, and one draw needn't show every extreme that they name: Text position j of prompt b in half c is a real token only if j < text_lengths[c, b]; in every draw some length equals 154 and some equals 1.
All inputs are finite; a program needn't handle non-finite values.
Results may differ from a plain program's by a relative error of at most 0.0085.
Values may be sent and summed in bfloat16 or wider, within the bound.
A program may use at most 128 MiB of HBM per device.

v0:
```python
import math
import jax
import jax.numpy as jnp
from jax import lax
from jax.sharding import PartitionSpec as P

HEAD_DIM = 64
TXT = 154
STEPS = 28
EPS = 1e-06
GUIDE = 4.5
SHIFT = 3.0


def partner_2(block, axis, stride):
    count = lax.axis_size(axis)
    route = []
    for low in range(count):
        high = low | 1 << stride
        if high != low and high < count:
            route += [(low, high), (high, low)]
    return lax.ppermute(block, axis, route)


def layer_norm(values):
    mean = jnp.mean(values, axis=-1, keepdims=True)
    centred = values - mean
    spread = jnp.mean(centred * centred, axis=-1, keepdims=True)
    return centred * lax.rsqrt(spread + EPS)


def modulate(values, shift, scale):
    return layer_norm(values) * (1.0 + scale) + shift


def head_norm(values, gain):
    shaped = values.reshape(values.shape[:-1] + (values.shape[-1] // HEAD_DIM, HEAD_DIM))
    square = jnp.mean(shaped * shaped, axis=-1, keepdims=True)
    return (shaped * lax.rsqrt(square + EPS) * gain).astype(jnp.bfloat16)


def sigma_of(index):
    level = 1.0 - index.astype(jnp.float32) / STEPS
    return SHIFT * level / (1.0 + (SHIFT - 1.0) * level)


def project_image(normed_rows, w_qkv, norm_gain):
    query = head_norm(
        jnp.einsum("tbd,de->tbe", normed_rows, w_qkv[0], preferred_element_type=jnp.float32),
        norm_gain[0],
    )
    keys = head_norm(
        jnp.einsum("tbd,de->tbe", normed_rows, w_qkv[1], preferred_element_type=jnp.float32),
        norm_gain[1],
    )
    values = jnp.einsum(
        "tbd,de->tbe", normed_rows, w_qkv[2], preferred_element_type=jnp.float32
    ).astype(jnp.bfloat16)
    flat_query = query.reshape(query.shape[:-2] + (-1,))
    flat_keys = keys.reshape(keys.shape[:-2] + (-1,))
    return jnp.concatenate([flat_query, flat_keys, values], axis=-1)


def key_terms(query, key_rows, value_rows, keep):
    factor = 1.0 / math.sqrt(HEAD_DIM)
    prompts = query.shape[1]
    if keep is None:
        keep = jnp.ones((prompts, key_rows.shape[0]), jnp.float32)

    def one_prompt(items):
        query_rows, keys_one, values_one, keep_one = items
        scores = (
            jnp.einsum("qhd,khd->hqk", query_rows, keys_one, preferred_element_type=jnp.float32)
            * factor
        )
        weights = jnp.exp(scores) * keep_one[None, None, :]
        numer = jnp.einsum(
            "hqk,khd->hqd",
            weights.astype(jnp.bfloat16),
            values_one,
            preferred_element_type=jnp.float32,
        )
        return (numer, jnp.sum(weights, axis=-1))

    return lax.map(
        one_prompt,
        (
            jnp.moveaxis(query, 1, 0),
            jnp.moveaxis(key_rows, 1, 0),
            jnp.moveaxis(value_rows, 1, 0),
            keep,
        ),
    )


def shards(
    image_hidden,
    text_hidden,
    modulation,
    text_lengths,
    timestep,
    latent,
    w_qkv,
    w_out,
    w_text_kv,
    norm_gain,
    w_up,
    w_down,
    w_head,
):
    mods = modulation[0]
    own_hidden = image_hidden[0]
    rows = own_hidden.shape[0]
    width = w_out.shape[0]
    heads = width // HEAD_DIM
    prompts = mods.shape[0]
    offset = lax.axis_index("mlp") * rows
    block_hidden = lax.all_gather(own_hidden, "mlp", axis=0, tiled=True).astype(jnp.float32)
    normed = modulate(block_hidden, mods[:, 0], mods[:, 1]).astype(jnp.bfloat16)
    projected = project_image(normed, w_qkv, norm_gain)
    block_rows = projected.shape[0]
    query = projected[..., :width].reshape(block_rows, prompts, heads, HEAD_DIM)
    own_pairs = projected[..., width:]
    text_rows = text_hidden.shape[1]
    position = lax.axis_index("seq") * text_rows + lax.iota(jnp.int32, text_rows)
    owner = position // TXT
    pick = (owner[:, None] == lax.iota(jnp.int32, prompts)[None, :]).astype(jnp.float32)
    text_shift = jnp.dot(pick, mods[:, 6], precision=lax.Precision.HIGHEST)
    text_scale = jnp.dot(pick, mods[:, 7], precision=lax.Precision.HIGHEST)
    text_normed = modulate(text_hidden[0].astype(jnp.float32), text_shift, text_scale).astype(
        jnp.bfloat16
    )
    text_keys = head_norm(
        jnp.dot(text_normed, w_text_kv[0], preferred_element_type=jnp.float32), norm_gain[2]
    )
    text_keys = text_keys.reshape(text_rows, width)
    text_values = jnp.dot(text_normed, w_text_kv[1], preferred_element_type=jnp.float32).astype(
        jnp.bfloat16
    )
    text_pairs = jnp.concatenate([text_keys, text_values], axis=-1)
    keep = (lax.iota(jnp.int32, TXT)[None, :] < text_lengths[0][:, None]).astype(jnp.float32)

    def split_pairs(pairs):
        shape = pairs.shape[:2] + (heads, HEAD_DIM)
        return (pairs[..., :width].reshape(shape), pairs[..., width:].reshape(shape))

    all_image, all_text = (
        lax.all_gather(own_pairs, "seq", axis=0, tiled=True),
        lax.all_gather(text_pairs, "seq", axis=0, tiled=True),
    )
    shaped = jnp.transpose(all_text.reshape(prompts, TXT, 2 * width), (1, 0, 2))
    key_rows, value_rows = split_pairs(shaped)
    text_numer, text_denom = key_terms(query, key_rows, value_rows, keep)
    key_rows, value_rows = split_pairs(all_image)
    image_numer, image_denom = key_terms(query, key_rows, value_rows, None)
    numer = text_numer + image_numer
    denom = text_denom + image_denom
    attended = (numer / denom[..., None]).astype(jnp.bfloat16)
    attended = jnp.transpose(attended, (2, 0, 1, 3)).reshape(block_rows, prompts, width)
    part = attended
    attention_out = lax.psum(
        jnp.einsum("tbe,ed->tbd", part, w_out, preferred_element_type=jnp.float32).astype(
            jnp.bfloat16
        ),
        "mlp",
    ).astype(jnp.float32)
    first = block_hidden + mods[:, 2] * attention_out
    mlp_in = modulate(first, mods[:, 3], mods[:, 4]).astype(jnp.bfloat16)
    raised = jnp.einsum("tbd,du->tbu", mlp_in, w_up, preferred_element_type=jnp.float32)
    activated = jax.nn.gelu(raised, approximate=True).astype(jnp.bfloat16)
    own_first = lax.dynamic_slice_in_dim(first, offset, rows, 0)
    part = activated
    mlp_out = lax.psum_scatter(
        jnp.einsum("tbu,ud->tbd", part, w_down, preferred_element_type=jnp.float32).astype(
            jnp.bfloat16
        ),
        "mlp",
        scatter_dimension=0,
        tiled=True,
    ).astype(jnp.float32)
    second = own_first + mods[:, 5] * mlp_out
    final = modulate(second, mods[:, 8], mods[:, 9]).astype(jnp.bfloat16)
    own_velocity = jnp.einsum("tbd,dp->tbp", final, w_head, preferred_element_type=jnp.float32)
    half_count = prompts // 2
    branch = lax.axis_index("cfg")
    outgoing = lax.dynamic_slice_in_dim(own_velocity, (1 - branch) * half_count, half_count, 1)
    kept = lax.dynamic_slice_in_dim(own_velocity, branch * half_count, half_count, 1)
    partner = partner_2(outgoing, "cfg", 0)
    is_conditional = branch == 0
    conditional = jnp.where(is_conditional, kept, partner)
    unconditional = jnp.where(is_conditional, partner, kept)
    velocity = unconditional + GUIDE * (conditional - unconditional)
    sigma_now = sigma_of(timestep[0])
    sigma_after = sigma_of(timestep[0] + 1)
    next_latent = latent + (sigma_after - sigma_now) * velocity
    denoised = latent - sigma_now * velocity
    return (velocity, next_latent, denoised)


def solution(mesh):
    placed = (
        P("cfg", ("seq", "mlp"), None, None),
        P("cfg", "seq", None),
        P("cfg", None, None, None),
        P("cfg", None),
        P(),
        P(("seq", "mlp"), "cfg", None),
        P(None, None, "mlp"),
        P("mlp", None),
        P(None, None, "mlp"),
        P(),
        P(None, "mlp"),
        P("mlp", None),
        P(),
    )
    return jax.shard_map(
        shards,
        mesh=mesh,
        in_specs=placed,
        out_specs=(
            P(("seq", "mlp"), "cfg", None),
            P(("seq", "mlp"), "cfg", None),
            P(("seq", "mlp"), "cfg", None),
        ),
        check_vma=False,
    )
```

profile of v0, /device:TPU:0, one launch (start us, length us, event | category | flops | bytes accessed | tf_op | source)
XLA Modules:
  0.0 328.8 jit_solution(14662058543458932708)
XLA Ops:
  14.3 3.2 slice_bitcast_fusion.1
  17.5 4.3 %copy.71 = bf16[768,1536]{1,0:T(8,128)(2,1)} copy(bf16[768,1536]{0,1:T(8,128)(2,1)} %slice_bitcast_fusion.1) | data formatting | bytes 4718592 | tf_op jit(solution)/shard_map/dot_general | solution.py:134
  21.8 2.4 fusion.64
  26.2 4.8 %slice_bitcast_fusion = (bf16[768,1536]{0,1:T(8,128)(2,1)}, bf16[768,1536]{0,1:T(8,128)(2,1)}) fusion(bf16[3,1536,768]{2,1,0:T(8,128)(2,1)} %param.23), kind=kLoop, calls=%fused_computation.55 | loop fusion | bytes 9437184 | tf_op jit(solution)/shard_map/tbd,de->tbe/dot_general | solution.py:53
  31.1 4.4 %copy.75 = bf16[768,1536]{1,0:T(8,128)(2,1)} copy(bf16[768,1536]{0,1:T(8,128)(2,1)} %get-tuple-element.177) | data formatting | bytes 4718592 | tf_op jit(solution)/shard_map/tbd,de->tbe/dot_general | solution.py:53
  35.4 12.9 %all-gather = bf16[1,32,8,1536]{3,2,0,1:T(8,128)(2,1)S(1)} all-gather(bf16[1,16,8,1536]{3,2,0,1:T(8,128)(2,1)S(1)} %bitcast.270), channel_id=2, replica_groups=mesh['cfg'=2,'seq'=8,'mlp'=2] {'mlp'}, dimensions={1}, use_global_device_ids=true | all-gather | bytes 1179648 | tf_op jit(solution)/shard_map/all_gather | solution.py:118
  49.6 2.7 multiply_reduce_fusion.1
  57.7 2.6 fusion.61
  61.6 4.4 %copy.68 = bf16[768,1536]{1,0:T(8,128)(2,1)} copy(bf16[768,1536]{0,1:T(8,128)(2,1)} %get-tuple-element.178) | data formatting | bytes 4718592 | tf_op jit(solution)/shard_map/tbd,de->tbe/dot_general | solution.py:49
  66.0 4.3 %multiply_reduce_fusion.2 = (f32[32,8,12]{1,2,0:T(8,128)S(1)}, f32[32,8,12,64]{3,1,2,0:T(8,128)}) fusion(bf16[12,64,1536,1]{2,1,0,3:T(8,128)(2,1)} %bitcast.264, f32[8,1536]{1,0:T(8,128)S(1)} %copy-done.16, f32[8,1536]{1,0:T(8,128)S(1)} %copy-done.18, f32[32,8]{1,0:T(8,128)S(1)} %copy-done.20, f32[32,8]{1,0:T(8,128)S(1)} %broadcast_multiply_fusion.1, ...), kind=kOutput, calls=%fused_computation.77 | convolution fusion | flops 606729216 | bytes 4044800 | tf_op jit(solution)/shard_map/tbd,de->tbe/dot_general | solution.py:49
  73.8 25.3 %all-gather.7.cloned.1.call-done = bf16[8,154,1536]{2,1,0:T(8,128)(2,1)} async-done(((bf16[1,154,1536]{2,1,0:T(8,128)(2,1)}), bf16[8,154,1536]{2,1,0:T(8,128)(2,1)}) %all-gather.7.cloned.1.call-update) | async-done | bytes 3784720 | tf_op jit(solution)/shard_map/all_gather | solution.py:149
  99.1 7.8 %copy.73 = bf16[8,154,1536]{1,2,0:T(8,128)(2,1)} copy(bf16[8,154,1536]{2,1,0:T(8,128)(2,1)} %all-gather.7.cloned.1.call-done) | data formatting | bytes 7569408 | tf_op jit(solution)/shard_map/all_gather | solution.py:149
  106.9 6.5 %fusion.100 = (bf16[154,8,768]{0,2,1:T(8,128)(2,1)}, bf16[154,8,768]{0,2,1:T(8,128)(2,1)}) fusion(bf16[154,8,1536]{0,2,1:T(8,128)(2,1)} %bitcast.258), kind=kLoop, calls=%fused_computation.149 | loop fusion | bytes 7569408 | tf_op jit(solution)/shard_map/slice | solution.py:145
  114.8 26.2 %while.24 = (s32[]{:T(128)}, f32[8,12,32,64]{3,2,1,0:T(8,128)}, f32[8,12,32]{2,1,0:T(8,128)S(1)}, bf16[8,32,12,64]{3,1,2,0:T(8,128)(2,1)}, bf16[8,154,12,64]{1,3...) while((s32[]{:T(128)}, f32[8,12,32,64]{3,2,1,0:T(8,128)}, ...), condition=%wide.region_8.9_spmd, body=%wide.region_6.8_spmd.sunk | while | flops 15374978 | bytes 1339797 | solution.py:85
  116.1 1.9 fusion.120
  119.4 1.9 fusion.120
  129.3 1.9 fusion.120
  132.5 1.9 fusion.120
  135.8 1.9 fusion.120
  141.0 57.7 %all-gather.5.cloned.1.call-done = bf16[256,8,1536]{2,1,0:T(8,128)(2,1)} async-done(((bf16[32,8,1536]{2,1,0:T(8,128)(2,1)}), bf16[256,8,1536]{2,1,0:T(8,128)(2,1)}) %all-gather.5.cloned.1.call-update) | async-done | bytes 6291472 | tf_op jit(solution)/shard_map/all_gather | solution.py:148
  198.7 5.9 %fusion.99 = (bf16[256,8,768]{2,1,0:T(8,128)(2,1)}, bf16[256,8,768]{2,1,0:T(8,128)(2,1)}) fusion(bf16[256,8,1536]{2,1,0:T(8,128)(2,1)} %all-gather.5.cloned.1.call-done), kind=kLoop, calls=%fused_computation.148 | loop fusion | bytes 12582912 | tf_op jit(solution)/shard_map/slice | solution.py:145
  204.6 5.0 %copy.84 = bf16[256,8,768]{0,2,1:T(8,128)(2,1)} copy(bf16[256,8,768]{2,1,0:T(8,128)(2,1)} %get-tuple-element.180) | data formatting | bytes 6291456
  209.6 5.0 %copy.85 = bf16[256,8,768]{0,2,1:T(8,128)(2,1)} copy(bf16[256,8,768]{2,1,0:T(8,128)(2,1)} %get-tuple-element.179) | data formatting | bytes 6291456
  215.9 26.0 %while.25 = (s32[]{:T(128)}, f32[8,12,32,64]{3,2,1,0:T(8,128)}, f32[8,12,32]{2,1,0:T(8,128)S(1)}, bf16[8,32,12,64]{3,1,2,0:T(8,128)(2,1)}, bf16[8,256,12,64]{1,3...) while((s32[]{:T(128)}, f32[8,12,32,64]{3,2,1,0:T(8,128)}, f32[8,12,32]{2,1,0:T(8,128)S(1)}, ...), condition=%wide.region_12.13_spmd, body=%wide.region_10.12_spmd.sunk | while | flops 25460352 | bytes 1494609 | solution.py:85
  220.5 1.9 fusion.124
  223.8 1.9 fusion.124
  230.3 1.9 fusion.124
  241.9 2.4 fusion.79
  249.5 32.4 %all-reduce.2.cloned.1.call-done = bf16[32,8,1536]{2,1,0:T(8,128)(2,1)} async-done(((bf16[32,8,1536]{2,1,0:T(8,128)(2,1)}), bf16[32,8,1536]{2,1,0:T(8,128)(2,1)}) %all-reduce.2.cloned.1.call-update) | async-done | bytes 786448 | tf_op jit(solution)/shard_map/psum | solution.py:161
  284.3 7.0 %fusion.36 = bf16[32,8,3072]{2,1,0:T(8,128)(2,1)S(1)} fusion(bf16[1536,3072]{1,0:T(8,128)(2,1)} %param.27, f32[32,8,1536]{2,1,0:T(8,128)S(1)} %get-tuple-element.172, f32[8,1536]{1,0:T(8,128)S(1)} %copy-done.13, f32[8,1536]{1,0:T(8,128)S(1)} %copy-done.14, f32[32,8]{1,0:T(8,128)S(1)} %add_rsqrt_fusion.1, f32[32,8]{1,0:T(8,128)S(1)} %broadcast_multiply_fusion), kind=kOutput, calls=%fused_computation.42 | convolution fusion | flops 2424963072 | bytes 12683264 | tf_op jit(solution)/shard_map/tbd,du->tbu/dot_general | solution.py:169
  291.3 7.2 %fusion.39 = bf16[32,8,1536]{2,1,0:T(8,128)(2,1)} fusion(bf16[32,8,3072]{2,1,0:T(8,128)(2,1)S(1)} %fusion.36, bf16[3072,1536]{1,0:T(8,128)(2,1)} %param.28), kind=kOutput, calls=%fused_computation.43 | convolution fusion | flops 2416312320 | bytes 11796480 | tf_op jit(solution)/shard_map/tbu,ud->tbd/dot_general | solution.py:174
  298.6 17.6 %reduce-scatter.2.cloned.1.call-done = bf16[16,8,1536]{2,1,0:T(8,128)(2,1)} async-done(((bf16[32,8,1536]{2,1,0:T(8,128)(2,1)}), bf16[16,8,1536]{2,1,0:T(8,128)(2,1)}) %reduce-scatter.2.cloned.1.call-update) | async-done | bytes 393232 | tf_op jit(solution)/shard_map/reduce_scatter | solution.py:173
  (159 shorter events, 72.6 us)
Async XLA Ops:
  7.2 240.4 %copy-start = (bf16[768,1536]{1,0:T(8,128)(2,1)S(1)}, bf16[768,1536]{1,0:T(8,128)(2,1)}, u32[]{:S(2)}) copy-start(bf16[768,1536]{1,0:T(8,128)(2,1)} %param.24) | copy-start | bytes 7077892
  7.2 91.9 %all-gather.7.cloned.1.call-start = ((), (), s32[]{:S(2)}) async-start(), calls=%async_computation.4 | async-start | bytes 4423680 | tf_op jit(solution)/shard_map/all_gather | solution.py:149
  21.8 2.4 copy-start.4
  26.2 172.5 %all-gather.5.cloned.1.call-start = ((), (), s32[]{:S(2)}) async-start(), calls=%async_computation.1 | async-start | bytes 7077888 | tf_op jit(solution)/shard_map/all_gather | solution.py:148
  31.1 4.4 %copy-start.8 = (bf16[1,16,8,1536]{3,2,1,0:T(8,128)(2,1)S(1)}, bf16[1,16,8,1536]{3,2,1,0:T(8,128)(2,1)}, u32[]{:S(2)}) copy-start(bf16[1,16,8,1536]{3,2,1,0:T(8,128)(2,1)} %param.17) | copy-start | bytes 1179652
  35.4 13.4 %copy-start.6 = (f32[1,8,10,1536]{3,1,2,0:T(8,128)S(1)}, f32[1,8,10,1536]{3,1,2,0:T(8,128)}, u32[]{:S(2)}) copy-start(f32[1,8,10,1536]{3,1,2,0:T(8,128)} %param.19) | copy-start | bytes 1474564
  35.4 14.2 %copy-start.3 = (bf16[768,1536]{1,0:T(8,128)(2,1)S(1)}, bf16[768,1536]{1,0:T(8,128)(2,1)}, u32[]{:S(2)}) copy-start(bf16[768,1536]{1,0:T(8,128)(2,1)} %copy.75) | copy-start | bytes 7077892
  48.8 3.5 %copy-start.19 = (f32[32,8]{1,0:T(8,128)}, f32[32,8]{1,0:T(8,128)S(1)}, u32[]{:S(2)}) copy-start(f32[32,8]{1,0:T(8,128)S(1)} %add_rsqrt_fusion.3) | copy-start | bytes 3076
  49.6 2.7 copy-start.15
  49.6 2.7 copy-start.17
  49.6 3.1 copy-start.22
  61.3 220.6 %all-reduce.2.cloned.1.call-start = ((), (), s32[]{:S(2)}) async-start(), calls=%async_computation.2 | async-start | bytes 1572864 | tf_op jit(solution)/shard_map/psum | solution.py:161
  61.5 4.5 %copy-start.16 = (f32[8,1536]{1,0:T(8,128)S(1)}, f32[8,1536]{1,0:T(8,128)}, u32[]{:S(2)}) copy-start(f32[8,1536]{1,0:T(8,128)} %copy-done.15) | copy-start | bytes 147460
  61.6 4.5 %copy-start.18 = (f32[8,1536]{1,0:T(8,128)S(1)}, f32[8,1536]{1,0:T(8,128)}, u32[]{:S(2)}) copy-start(f32[8,1536]{1,0:T(8,128)} %copy-done.17) | copy-start | bytes 147460
  61.6 4.5 %copy-start.20 = (f32[32,8]{1,0:T(8,128)S(1)}, f32[32,8]{1,0:T(8,128)}, u32[]{:S(2)}) copy-start(f32[32,8]{1,0:T(8,128)} %copy-done.19) | copy-start | bytes 3076
  66.0 4.6 %copy-start.21 = (f32[64]{0:T(128)S(1)}, f32[64]{0:T(128)}, u32[]{:S(2)}) copy-start(f32[64]{0:T(128)} %get-tuple-element.192) | copy-start | bytes 772
  70.7 3.1 copy-start.23
  249.3 66.9 %reduce-scatter.2.cloned.1.call-start = ((), (), s32[]{:S(2)}) async-start(), calls=%async_computation.3 | async-start | bytes 1179648 | tf_op jit(solution)/shard_map/reduce_scatter | solution.py:173
  283.4 7.9 %copy-start.1 = (f32[32,8,1536]{2,1,0:T(8,128)}, f32[32,8,1536]{2,1,0:T(8,128)S(1)}, u32[]{:S(2)}) copy-start(f32[32,8,1536]{2,1,0:T(8,128)S(1)} %get-tuple-element.172) | copy-start | bytes 4718596
  283.4 0.8 copy-start.13
  283.4 0.9 copy-start.14
  291.3 24.9 %copy-start.7 = (f32[8,1536]{1,0:T(8,128)S(1)}, f32[8,1536]{1,0:T(8,128)}, u32[]{:S(2)}) copy-start(f32[8,1536]{1,0:T(8,128)} %get-tuple-element.183) | copy-start | bytes 147460
  298.5 20.7 %copy-start.11 = (f32[8,1536]{1,0:T(8,128)S(1)}, f32[8,1536]{1,0:T(8,128)}, u32[]{:S(2)}) copy-start(f32[8,1536]{1,0:T(8,128)} %get-tuple-element.184) | copy-start | bytes 147460
  298.6 20.7 %copy-start.12 = (f32[8,1536]{1,0:T(8,128)S(1)}, f32[8,1536]{1,0:T(8,128)}, u32[]{:S(2)}) copy-start(f32[8,1536]{1,0:T(8,128)} %get-tuple-element.185) | copy-start | bytes 147460
  298.6 20.7 %copy-start.24 = (bf16[1536,64]{0,1:T(8,128)(2,1)S(1)}, bf16[1536,64]{0,1:T(8,128)(2,1)}, u32[]{:S(2)}) copy-start(bf16[1536,64]{0,1:T(8,128)(2,1)} %param.29) | copy-start | bytes 589828
  316.2 3.1 copy-start.2
  316.2 3.1 copy-start.5
  317.8 3.2 copy-start.9
  319.7 1.3 collective-permute-start
  321.6 0.6 copy-start.10
Sparse Core Ops, SparseCore 0:
  26.3 72.7 all-gather.6
  101.3 97.3 all-gather.4
  249.4 32.4 all-reduce.1
  298.7 17.4 reduce-scatter.1
where the time goes:
time: 331 us; the launch traced here: 329 us
  waiting for transfers between devices  133 us (40%)
  matrix products  84.2 us (25%)
  local copies, waits for them, and re-layouts  64.4 us (19%)
  other arithmetic  18.2 us (5%)
  between operations  14.9 us (5%)
  blocking collectives  12.9 us (4%)
    all_gather x1, waiting for transfers between devices, shards(): lax.all_gather(own_pairs, 'seq', axis=0, tiled=True)  57.7 us
    psum x1, waiting for transfers between devices, shards(): lax.psum(jnp.einsum('tbe,ed->tbd', part, w_out, preferred_element_type=jn...  32.4 us
    dot_general x16, matrix products, one_prompt(): jnp.einsum('hqk,khd->hqd', weights.astype(jnp.bfloat16), values_one, pref...  30.6 us
    all_gather x1, waiting for transfers between devices, shards(): lax.all_gather(text_pairs, 'seq', axis=0, tiled=True)  25.3 us
    dot_general x16, matrix products, one_prompt(): jnp.einsum('qhd,khd->hqk', query_rows, keys_one, preferred_element_type=j...  21.4 us
    reduce_scatter x1, waiting for transfers between devices, shards(): lax.psum_scatter(jnp.einsum('tbu,ud->tbd', part, w_down, preferred_elemen...  17.6 us
    all_gather x1, blocking collectives, shards(): lax.all_gather(own_hidden, 'mlp', axis=0, tiled=True).astype(jnp.float32)  12.9 us
    slice x2, local copies, waits for them, and re-layouts, split_pairs(): pairs[..., width:].reshape(shape)  12.4 us
  transfers between devices with their start and end apart: 5, of which 5 were waited for; matrix products, arithmetic and copies ran while one was open for 23% of the time, Pallas kernels for 0%

commit v1 on v0

--- a/solution.py
+++ b/solution.py
@@ -144,8 +144,27 @@
         shape = pairs.shape[:2] + (heads, HEAD_DIM)
         return (pairs[..., :width].reshape(shape), pairs[..., width:].reshape(shape))
 
+    def drive_strings(mine):
+        chip_axis = "seq"
+        current_value = jax.lax.axis_size(chip_axis)
+        even = jax.lax.axis_index(chip_axis)
+        mixed_arr, main, ready = (current_value, even, mine.shape[0])
+        lower = jnp.zeros(
+            [c * mixed_arr if no == 0 else c for no, c in enumerate(mine.shape)], mine.dtype
+        )
+        s_next = lax.dynamic_update_slice_in_dim(lower, mine, main * ready, axis=0)
+        for jj in range(1, mixed_arr):
+            spare = range(mixed_arr)
+            p_next = map(lambda no: (no, (no + 1) % mixed_arr), spare)
+            after = list(p_next)
+            mine = jax.lax.ppermute(mine, chip_axis, after)
+            s_next = lax.dynamic_update_slice_in_dim(
+                s_next, mine, (main - jj) % mixed_arr * ready, axis=0
+            )
+        return s_next
+
     all_image, all_text = (
-        lax.all_gather(own_pairs, "seq", axis=0, tiled=True),
+        drive_strings(own_pairs),
         lax.all_gather(text_pairs, "seq", axis=0, tiled=True),
     )
     shaped = jnp.transpose(all_text.reshape(prompts, TXT, 2 * width), (1, 0, 2))

time: 331 us -> 642 us (1.94); the launches traced: 329 us -> 633 us
  local copies, waits for them, and re-layouts: 64.4 us -> 354 us
  waiting for transfers between devices: 133 us -> 146 us
    dynamic_update_slice x0 -> x8, local copies, waits for them, and re-layouts: none -> 266 us  [the longest x7 236 us: drive_strings(): lax.dynamic_update_slice_in_dim(s_next, mine, (main - jj) % mixed_arr * r...]
    ppermute x0 -> x7, waiting for transfers between devices: none -> 93.1 us  [drive_strings(): mine = jax.lax.ppermute(mine, chip_axis, after)]
    all_gather x1 -> x0, waiting for transfers between devices: 57.7 us -> none  [shards(): lax.all_gather(own_pairs, 'seq', axis=0, tiled=True)]
    ppermute x0 -> x7, local copies, waits for them, and re-layouts: none -> 27.3 us  [drive_strings(): mine = jax.lax.ppermute(mine, chip_axis, after)]
    all_gather x1, waiting for transfers between devices: 25.3 us -> 0.01 us  [shards(): lax.all_gather(text_pairs, 'seq', axis=0, tiled=True)]
    unnamed x52 -> x60, local copies, waits for them, and re-layouts: 10.7 us -> 0.69 us
  transfers between devices with their start and end apart: 5 -> 11, of which waited for: 5 -> 9; matrix products, arithmetic and copies ran while one was open for 23% -> 57% of each run, Pallas kernels for 0% -> 0%
where the time goes in v1:
time: 642 us; the launch traced here: 633 us
  local copies, waits for them, and re-layouts  354 us (55%)
  waiting for transfers between devices  146 us (23%)
  matrix products  85.2 us (13%)
  other arithmetic  17.3 us (3%)
  between operations  14.9 us (2%)
  blocking collectives  13.1 us (2%)
    dynamic_update_slice x7, local copies, waits for them, and re-layouts, drive_strings(): lax.dynamic_update_slice_in_dim(s_next, mine, (main - jj) % mixed_arr * r...  236 us
    ppermute x7, waiting for transfers between devices, drive_strings(): mine = jax.lax.ppermute(mine, chip_axis, after)  93.1 us
    psum x1, waiting for transfers between devices, shards(): lax.psum(jnp.einsum('tbe,ed->tbd', part, w_out, preferred_element_type=jn...  35 us
    dot_general x16, matrix products, one_prompt(): jnp.einsum('hqk,khd->hqd', weights.astype(jnp.bfloat16), values_one, pref...  30.7 us
    dynamic_update_slice x1, local copies, waits for them, and re-layouts, drive_strings(): s_next = lax.dynamic_update_slice_in_dim(lower, mine, main * ready, axis=0)  30.2 us
    ppermute x7, local copies, waits for them, and re-layouts, drive_strings(): mine = jax.lax.ppermute(mine, chip_axis, after)  27.3 us
    dot_general x16, matrix products, one_prompt(): jnp.einsum('qhd,khd->hqk', query_rows, keys_one, preferred_element_type=j...  21.4 us
    reduce_scatter x1, waiting for transfers between devices, shards(): lax.psum_scatter(jnp.einsum('tbu,ud->tbd', part, w_down, preferred_elemen...  17.6 us
  transfers between devices with their start and end apart: 11, of which 9 were waited for; matrix products, arithmetic and copies ran while one was open for 57% of the time, Pallas kernels for 0%

profile of v1, /device:TPU:0, one launch (start us, length us, event | category | flops | bytes accessed | tf_op | source)
XLA Modules:
  0.0 633.3 jit_solution(16348302127439707476)
XLA Ops:
  7.2 13.1 %all-gather = bf16[1,32,8,1536]{3,2,0,1:T(8,128)(2,1)S(1)} all-gather(bf16[1,16,8,1536]{3,2,0,1:T(8,128)(2,1)} %bitcast.270), channel_id=2, replica_groups=mesh['cfg'=2,'seq'=8,'mlp'=2] {'mlp'}, dimensions={1}, use_global_device_ids=true | all-gather | bytes 1179648 | tf_op jit(solution)/shard_map/all_gather | solution.py:118
  21.6 4.9 slice_bitcast_fusion
  26.5 4.3 copy.99
  45.7 19.7 %collective-permute-done = bf16[32,8,1536]{2,1,0:T(8,128)(2,1)S(1)} collective-permute-done((bf16[32,8,1536]{2,1,0:T(8,128)(2,1)S(1)}, bf16[32,8,1536]{2,1,0:T(8,128)(2,1)S(1)}, u32[]{:S(2)}, u32[]{:S(2)}) %collective-permute-start) | collective-permute-done | bytes 786464 | tf_op jit(solution)/shard_map/ppermute | solution.py:160
  65.6 20.4 %collective-permute-done.1 = bf16[32,8,1536]{2,1,0:T(8,128)(2,1)} collective-permute-done((bf16[32,8,1536]{2,1,0:T(8,128)(2,1)S(1)}, bf16[32,8,1536]{2,1,0:T(8,128)(2,1)}, u32[]{:S(2)}, u32[]{:S(2)}) %collective-permute-start.1) | collective-permute-done | bytes 786464 | tf_op jit(solution)/shard_map/ppermute | solution.py:160
  90.6 15.3 %collective-permute-done.2 = bf16[32,8,1536]{2,1,0:T(8,128)(2,1)} collective-permute-done((bf16[32,8,1536]{2,1,0:T(8,128)(2,1)}, bf16[32,8,1536]{2,1,0:T(8,128)(2,1)}, u32[]{:S(2)}, u32[]{:S(2)}) %collective-permute-start.2) | collective-permute-done | bytes 786464 | tf_op jit(solution)/shard_map/ppermute | solution.py:160
  105.9 4.3 copy.95
  113.5 11.3 %collective-permute-done.3 = bf16[32,8,1536]{2,1,0:T(8,128)(2,1)} collective-permute-done((bf16[32,8,1536]{2,1,0:T(8,128)(2,1)}, bf16[32,8,1536]{2,1,0:T(8,128)(2,1)}, u32[]{:S(2)}, u32[]{:S(2)}) %collective-permute-start.3) | collective-permute-done | bytes 786464 | tf_op jit(solution)/shard_map/ppermute | solution.py:160
  126.7 16.1 %collective-permute-done.4 = bf16[32,8,1536]{2,1,0:T(8,128)(2,1)} collective-permute-done((bf16[32,8,1536]{2,1,0:T(8,128)(2,1)}, bf16[32,8,1536]{2,1,0:T(8,128)(2,1)}, u32[]{:S(2)}, u32[]{:S(2)}) %collective-permute-start.4) | collective-permute-done | bytes 786464 | tf_op jit(solution)/shard_map/ppermute | solution.py:160
  146.1 4.3 copy.92
  150.4 10.3 %collective-permute-done.5 = bf16[32,8,1536]{2,1,0:T(8,128)(2,1)} collective-permute-done((bf16[32,8,1536]{2,1,0:T(8,128)(2,1)}, bf16[32,8,1536]{2,1,0:T(8,128)(2,1)}, u32[]{:S(2)}, u32[]{:S(2)}) %collective-permute-start.5) | collective-permute-done | bytes 786464 | tf_op jit(solution)/shard_map/ppermute | solution.py:160
  160.7 4.3 multiply_reduce_fusion.2
  165.0 3.9 copy.103
  175.5 30.2 %dynamic_update_slice.38 = bf16[256,8,1536]{0,2,1:T(8,128)(2,1)} dynamic-update-slice(bf16[256,8,1536]{0,2,1:T(8,128)(2,1)} %broadcast_in_dim.15, bf16[32,8,1536]{0,2,1:T(8,128)(2,1)} %copy.103, s32[]{:T(128)S(6)} %select_n.87, s32[]{:T(128)} %constant.153.clone.1, s32[]{:T(128)} %constant.153.clone.1) | dynamic-update-slice | bytes 1572868 | tf_op jit(solution)/shard_map/dynamic_update_slice | solution.py:155
  205.7 3.9 copy.104
  209.6 34.0 %dynamic_update_slice.39 = bf16[256,8,1536]{0,2,1:T(8,128)(2,1)} dynamic-update-slice(bf16[256,8,1536]{0,2,1:T(8,128)(2,1)} %dynamic_update_slice.38, bf16[32,8,1536]{0,2,1:T(8,128)(2,1)} %copy.104, s32[]{:T(128)S(6)} %select_n.89, s32[]{:T(128)} %constant.153.clone.1, s32[]{:T(128)} %constant.153.clone.1) | dynamic-update-slice | bytes 1572868 | tf_op jit(solution)/shard_map/dynamic_update_slice | solution.py:161
  247.5 34.0 %dynamic_update_slice.40 = bf16[256,8,1536]{0,2,1:T(8,128)(2,1)} dynamic-update-slice(bf16[256,8,1536]{0,2,1:T(8,128)(2,1)} %dynamic_update_slice.39, bf16[32,8,1536]{0,2,1:T(8,128)(2,1)} %copy.105, s32[]{:T(128)S(6)} %select_n.91, s32[]{:T(128)} %constant.153.clone.1, s32[]{:T(128)} %constant.153.clone.1) | dynamic-update-slice | bytes 1572868 | tf_op jit(solution)/shard_map/dynamic_update_slice | solution.py:161
  285.4 34.0 %dynamic_update_slice.41 = bf16[256,8,1536]{0,2,1:T(8,128)(2,1)} dynamic-update-slice(bf16[256,8,1536]{0,2,1:T(8,128)(2,1)} %dynamic_update_slice.40, bf16[32,8,1536]{0,2,1:T(8,128)(2,1)} %copy.106, s32[]{:T(128)S(6)} %select_n.93, s32[]{:T(128)} %constant.153.clone.1, s32[]{:T(128)} %constant.153.clone.1) | dynamic-update-slice | bytes 1572868 | tf_op jit(solution)/shard_map/dynamic_update_slice | solution.py:161
  323.4 28.9 %dynamic_update_slice.42 = bf16[256,8,1536]{0,2,1:T(8,128)(2,1)} dynamic-update-slice(bf16[256,8,1536]{0,2,1:T(8,128)(2,1)} %dynamic_update_slice.41, bf16[32,8,1536]{0,2,1:T(8,128)(2,1)} %copy.107, s32[]{:T(128)S(6)} %select_n.95, s32[]{:T(128)} %constant.153.clone.1, s32[]{:T(128)} %constant.153.clone.1) | dynamic-update-slice | bytes 1572868 | tf_op jit(solution)/shard_map/dynamic_update_slice | solution.py:161
  356.2 35.0 %dynamic_update_slice.43 = bf16[256,8,1536]{0,2,1:T(8,128)(2,1)} dynamic-update-slice(bf16[256,8,1536]{0,2,1:T(8,128)(2,1)} %dynamic_update_slice.42, bf16[32,8,1536]{0,2,1:T(8,128)(2,1)} %copy.108, s32[]{:T(128)S(6)} %select_n.97, s32[]{:T(128)} %constant.153.clone.1, s32[]{:T(128)} %constant.153.clone.1) | dynamic-update-slice | bytes 1572868 | tf_op jit(solution)/shard_map/dynamic_update_slice | solution.py:161
  395.1 35.0 %dynamic_update_slice.44 = bf16[256,8,1536]{0,2,1:T(8,128)(2,1)} dynamic-update-slice(bf16[256,8,1536]{0,2,1:T(8,128)(2,1)} %dynamic_update_slice.43, bf16[32,8,1536]{0,2,1:T(8,128)(2,1)} %copy.109, s32[]{:T(128)S(6)} %select_n.99, s32[]{:T(128)} %constant.153.clone.1, s32[]{:T(128)} %constant.153.clone.1) | dynamic-update-slice | bytes 1572868 | tf_op jit(solution)/shard_map/dynamic_update_slice | solution.py:161
  430.1 3.9 copy.110
  434.0 35.0 %dynamic_update_slice.45 = bf16[256,8,1536]{0,2,1:T(8,128)(2,1)} dynamic-update-slice(bf16[256,8,1536]{0,2,1:T(8,128)(2,1)} %dynamic_update_slice.44, bf16[32,8,1536]{0,2,1:T(8,128)(2,1)} %copy.110, s32[]{:T(128)S(6)} %select_n.101, s32[]{:T(128)} %constant.153.clone.1, s32[]{:T(128)} %constant.153.clone.1) | dynamic-update-slice | bytes 1572868 | tf_op jit(solution)/shard_map/dynamic_update_slice | solution.py:161
  468.9 6.0 fusion.99
  476.3 26.1 %while.25 = (s32[]{:T(128)}, f32[8,12,32,64]{3,2,1,0:T(8,128)}, f32[8,12,32]{2,1,0:T(8,128)S(1)}, bf16[8,32,12,64]{3,1,2,0:T(8,128)(2,1)}, bf16[8,256,12,64]{1,3...) while((s32[]{:T(128)}, f32[8,12,32,64]{3,2,1,0:T(8,128)}, f32[8,12,32]{2,1,0:T(8,128)S(1)}, ...), condition=%wide.region_12.13_spmd, body=%wide.region_10.12_spmd.sunk | while | flops 25460352 | bytes 1494609 | solution.py:85
  502.4 7.7 %copy.97 = bf16[8,154,1536]{1,2,0:T(8,128)(2,1)} copy(bf16[8,154,1536]{2,1,0:T(8,128)(2,1)} %all-gather.4.cloned.1.call-done) | data formatting | bytes 7569408 | tf_op jit(solution)/shard_map/all_gather | solution.py:168
  510.1 6.0 fusion.100
  517.5 26.2 %while.24 = (s32[]{:T(128)}, f32[8,12,32,64]{3,2,1,0:T(8,128)}, f32[8,12,32]{2,1,0:T(8,128)S(1)}, bf16[8,32,12,64]{3,1,2,0:T(8,128)(2,1)}, bf16[8,154,12,64]{1,3...) while((s32[]{:T(128)}, f32[8,12,32,64]{3,2,1,0:T(8,128)}, ...), condition=%wide.region_8.9_spmd, body=%wide.region_6.8_spmd.sunk | while | flops 15374978 | bytes 1339797 | solution.py:85
  551.4 35.0 %all-reduce.2.cloned.1.call-done = bf16[32,8,1536]{2,1,0:T(8,128)(2,1)} async-done(((bf16[32,8,1536]{2,1,0:T(8,128)(2,1)}), bf16[32,8,1536]{2,1,0:T(8,128)(2,1)}) %all-reduce.2.cloned.1.call-update) | async-done | bytes 786448 | tf_op jit(solution)/shard_map/psum | solution.py:180
  588.8 7.0 %fusion.36 = bf16[32,8,3072]{2,1,0:T(8,128)(2,1)S(1)} fusion(bf16[1536,3072]{1,0:T(8,128)(2,1)} %param.27, f32[32,8,1536]{2,1,0:T(8,128)S(1)} %get-tuple-element.172, f32[8,1536]{1,0:T(8,128)S(1)} %copy-done.17, f32[8,1536]{1,0:T(8,128)S(1)} %copy-done.18, f32[32,8]{1,0:T(8,128)S(1)} %add_rsqrt_fusion.1, f32[32,8]{1,0:T(8,128)S(1)} %broadcast_multiply_fusion), kind=kOutput, calls=%fused_computation.42 | convolution fusion | flops 2424963072 | bytes 12683264 | tf_op jit(solution)/shard_map/tbd,du->tbu/dot_general | solution.py:188
  595.8 7.2 %fusion.39 = bf16[32,8,1536]{2,1,0:T(8,128)(2,1)} fusion(bf16[32,8,3072]{2,1,0:T(8,128)(2,1)S(1)} %fusion.36, bf16[3072,1536]{1,0:T(8,128)(2,1)} %param.28), kind=kOutput, calls=%fused_computation.43 | convolution fusion | flops 2416312320 | bytes 11796480 | tf_op jit(solution)/shard_map/tbu,ud->tbd/dot_general | solution.py:193
  603.1 17.6 %reduce-scatter.2.cloned.1.call-done = bf16[16,8,1536]{2,1,0:T(8,128)(2,1)} async-done(((bf16[32,8,1536]{2,1,0:T(8,128)(2,1)}), bf16[16,8,1536]{2,1,0:T(8,128)(2,1)}) %reduce-scatter.2.cloned.1.call-update) | async-done | bytes 393232 | tf_op jit(solution)/shard_map/reduce_scatter | solution.py:192
  (195 shorter events, 125.5 us)
Async XLA Ops:
  7.2 542.4 %copy-start = (bf16[768,1536]{1,0:T(8,128)(2,1)S(1)}, bf16[768,1536]{1,0:T(8,128)(2,1)}, u32[]{:S(2)}) copy-start(bf16[768,1536]{1,0:T(8,128)(2,1)} %param.24) | copy-start | bytes 7077892
  7.2 495.2 %all-gather.4.cloned.1.call-start = ((), (), s32[]{:S(2)}) async-start(), calls=%async_computation.3 | async-start | bytes 4423680 | tf_op jit(solution)/shard_map/all_gather | solution.py:168
  7.2 13.7 %copy-start.10 = (f32[1,8,10,1536]{3,1,2,0:T(8,128)S(1)}, f32[1,8,10,1536]{3,1,2,0:T(8,128)}, u32[]{:S(2)}) copy-start(f32[1,8,10,1536]{3,1,2,0:T(8,128)} %param.19) | copy-start | bytes 1474564
  20.9 13.3 %copy-start.23 = (f32[32,8]{1,0:T(8,128)}, f32[32,8]{1,0:T(8,128)S(1)}, u32[]{:S(2)}) copy-start(f32[32,8]{1,0:T(8,128)S(1)} %add_rsqrt_fusion.3) | copy-start | bytes 3076
  21.6 12.6 %copy-start.19 = (f32[8,1536]{1,0:T(8,128)}, f32[8,1536]{1,0:T(8,128)S(1)}, u32[]{:S(2)}) copy-start(f32[8,1536]{1,0:T(8,128)S(1)} %get-tuple-element.188) | copy-start | bytes 147460
  21.6 12.6 %copy-start.21 = (f32[8,1536]{1,0:T(8,128)}, f32[8,1536]{1,0:T(8,128)S(1)}, u32[]{:S(2)}) copy-start(f32[8,1536]{1,0:T(8,128)S(1)} %get-tuple-element.189) | copy-start | bytes 147460
  42.8 22.7 %copy-start.3 = (bf16[1,154,1536]{2,1,0:T(8,128)(2,1)S(1)}, bf16[1,154,1536]{2,1,0:T(8,128)(2,1)}, u32[]{:S(2)}) copy-start(bf16[1,154,1536]{2,1,0:T(8,128)(2,1)} %param.18) | copy-start | bytes 1419268
  43.9 21.7 %copy-start.4 = (bf16[32,8,1536]{2,1,0:T(8,128)(2,1)}, bf16[32,8,1536]{2,1,0:T(8,128)(2,1)S(1)}, u32[]{:S(2)}) copy-start(bf16[32,8,1536]{2,1,0:T(8,128)(2,1)S(1)} %pad_maximum_fusion) | copy-start | bytes 2359300
  43.9 21.5 %collective-permute-start = (bf16[32,8,1536]{2,1,0:T(8,128)(2,1)S(1)}, bf16[32,8,1536]{2,1,0:T(8,128)(2,1)S(1)}, u32[]{:S(2)}, u32[]{:S(2)}) collective-permute-start(bf16[32,8,1536]{2,1,0:T(8,128)(2,1)S(1)} %pad_maximum_fusion), channel_id=1, source_target_pairs={{0,2},{2,4},{4,6},{6,8},{8,10},{10,12},{12,14},{14,0},{1,3},{3,5},... | collective-permute-start | bytes 2359304 | tf_op jit(solution)/shard_map/ppermute | solution.py:160
  65.4 20.6 %copy-start.9 = (bf16[32,8,1536]{2,1,0:T(8,128)(2,1)}, bf16[32,8,1536]{2,1,0:T(8,128)(2,1)S(1)}, u32[]{:S(2)}) copy-start(bf16[32,8,1536]{2,1,0:T(8,128)(2,1)S(1)} %collective-permute-done) | copy-start | bytes 2359300
  65.4 20.6 %collective-permute-start.1 = (bf16[32,8,1536]{2,1,0:T(8,128)(2,1)S(1)}, bf16[32,8,1536]{2,1,0:T(8,128)(2,1)}, u32[]{:S(2)}, u32[]{:S(2)}) collective-permute-start(bf16[32,8,1536]{2,1,0:T(8,128)(2,1)S(1)} %collective-permute-done), channel_id=1, source_target_pairs={{0,2},{2,4},{4,6},{6,8},{8,10},{10,12},{12,14},{14,0},{1,3},{3,5},... | collective-permute-start | bytes 2359304 | tf_op jit(solution)/shard_map/ppermute | solution.py:160
  86.0 19.9 %collective-permute-start.2 = (bf16[32,8,1536]{2,1,0:T(8,128)(2,1)}, bf16[32,8,1536]{2,1,0:T(8,128)(2,1)}, u32[]{:S(2)}, u32[]{:S(2)}) collective-permute-start(bf16[32,8,1536]{2,1,0:T(8,128)(2,1)} %collective-permute-done.1), channel_id=1, source_target_pairs={{0,2},{2,4},{4,6},{6,8},{8,10},{10,12},{12,14},{14,0},{1,3},{3,5},... | collective-permute-start | bytes 2359304 | tf_op jit(solution)/shard_map/ppermute | solution.py:160
  105.8 18.9 %collective-permute-start.3 = (bf16[32,8,1536]{2,1,0:T(8,128)(2,1)}, bf16[32,8,1536]{2,1,0:T(8,128)(2,1)}, u32[]{:S(2)}, u32[]{:S(2)}) collective-permute-start(bf16[32,8,1536]{2,1,0:T(8,128)(2,1)} %collective-permute-done.2), channel_id=1, source_target_pairs={{0,2},{2,4},{4,6},{6,8},{8,10},{10,12},{12,14},{14,0},{1,3},{3,5},... | collective-permute-start | bytes 2359304 | tf_op jit(solution)/shard_map/ppermute | solution.py:160
  110.1 14.6 %copy-start.5 = (bf16[768,1536]{1,0:T(8,128)(2,1)S(1)}, bf16[768,1536]{1,0:T(8,128)(2,1)}, u32[]{:S(2)}) copy-start(bf16[768,1536]{1,0:T(8,128)(2,1)} %copy.95) | copy-start | bytes 7077892
  113.5 12.1 %copy-start.11 = (bf16[154,1536]{1,0:T(8,128)(2,1)}, bf16[154,1536]{1,0:T(8,128)(2,1)S(1)}, u32[]{:S(2)}) copy-start(bf16[154,1536]{1,0:T(8,128)(2,1)S(1)} %fusion.43) | copy-start | bytes 1419268
  124.8 18.0 %collective-permute-start.4 = (bf16[32,8,1536]{2,1,0:T(8,128)(2,1)}, bf16[32,8,1536]{2,1,0:T(8,128)(2,1)}, u32[]{:S(2)}, u32[]{:S(2)}) collective-permute-start(bf16[32,8,1536]{2,1,0:T(8,128)(2,1)} %collective-permute-done.3), channel_id=1, source_target_pairs={{0,2},{2,4},{4,6},{6,8},{8,10},{10,12},{12,14},{14,0},{1,3},{3,5},... | collective-permute-start | bytes 2359304 | tf_op jit(solution)/shard_map/ppermute | solution.py:160
  126.7 18.5 %copy-start.8 = (bf16[154,768]{1,0:T(8,128)(2,1)S(1)}, bf16[154,768]{1,0:T(8,128)(2,1)}, u32[]{:S(2)}) copy-start(bf16[154,768]{1,0:T(8,128)(2,1)} %copy.96) | copy-start | bytes 709636
  142.8 17.9 %collective-permute-start.5 = (bf16[32,8,1536]{2,1,0:T(8,128)(2,1)}, bf16[32,8,1536]{2,1,0:T(8,128)(2,1)}, u32[]{:S(2)}, u32[]{:S(2)}) collective-permute-start(bf16[32,8,1536]{2,1,0:T(8,128)(2,1)} %collective-permute-done.4), channel_id=1, source_target_pairs={{0,2},{2,4},{4,6},{6,8},{8,10},{10,12},{12,14},{14,0},{1,3},{3,5},... | collective-permute-start | bytes 2359304 | tf_op jit(solution)/shard_map/ppermute | solution.py:160
  146.0 440.4 %all-reduce.2.cloned.1.call-start = ((), (), s32[]{:S(2)}) async-start(), calls=%async_computation.1 | async-start | bytes 1572864 | tf_op jit(solution)/shard_map/psum | solution.py:180
  146.1 14.6 %copy-start.20 = (f32[8,1536]{1,0:T(8,128)S(1)}, f32[8,1536]{1,0:T(8,128)}, u32[]{:S(2)}) copy-start(f32[8,1536]{1,0:T(8,128)} %copy-done.19) | copy-start | bytes 147460
  146.1 14.6 %copy-start.22 = (f32[8,1536]{1,0:T(8,128)S(1)}, f32[8,1536]{1,0:T(8,128)}, u32[]{:S(2)}) copy-start(f32[8,1536]{1,0:T(8,128)} %copy-done.21) | copy-start | bytes 147460
  146.1 14.6 %copy-start.24 = (f32[32,8]{1,0:T(8,128)S(1)}, f32[32,8]{1,0:T(8,128)}, u32[]{:S(2)}) copy-start(f32[32,8]{1,0:T(8,128)} %copy-done.23) | copy-start | bytes 3076
  160.7 269.4 %collective-permute-start.6 = (bf16[32,8,1536]{2,1,0:T(8,128)(2,1)}, bf16[32,8,1536]{2,1,0:T(8,128)(2,1)}, u32[]{:S(2)}, u32[]{:S(2)}) collective-permute-start(bf16[32,8,1536]{2,1,0:T(8,128)(2,1)} %collective-permute-done.5), channel_id=1, source_target_pairs={{0,2},{2,4},{4,6},{6,8},{8,10},{10,12},{12,14},{14,0},{1,3},{3,5},... | collective-permute-start | bytes 2359304 | tf_op jit(solution)/shard_map/ppermute | solution.py:160
  165.0 4.2 copy-start.26
  175.5 30.2 %copy-start.28 = (s32[1,8]{1,0:T(1,128)S(1)}, s32[1,8]{1,0:T(1,128)}, u32[]{:S(2)}) copy-start(s32[1,8]{1,0:T(1,128)} %param.20) | copy-start | bytes 100
  551.3 69.4 %reduce-scatter.2.cloned.1.call-start = ((), (), s32[]{:S(2)}) async-start(), calls=%async_computation.2 | async-start | bytes 1179648 | tf_op jit(solution)/shard_map/reduce_scatter | solution.py:192
  587.9 7.9 %copy-start.1 = (f32[32,8,1536]{2,1,0:T(8,128)}, f32[32,8,1536]{2,1,0:T(8,128)S(1)}, u32[]{:S(2)}) copy-start(f32[32,8,1536]{2,1,0:T(8,128)S(1)} %get-tuple-element.172) | copy-start | bytes 4718596
  595.8 24.9 %copy-start.12 = (f32[8,1536]{1,0:T(8,128)S(1)}, f32[8,1536]{1,0:T(8,128)}, u32[]{:S(2)}) copy-start(f32[8,1536]{1,0:T(8,128)} %get-tuple-element.183) | copy-start | bytes 147460
  603.0 20.7 %copy-start.15 = (f32[8,1536]{1,0:T(8,128)S(1)}, f32[8,1536]{1,0:T(8,128)}, u32[]{:S(2)}) copy-start(f32[8,1536]{1,0:T(8,128)} %get-tuple-element.184) | copy-start | bytes 147460
  603.1 20.7 %copy-start.16 = (f32[8,1536]{1,0:T(8,128)S(1)}, f32[8,1536]{1,0:T(8,128)}, u32[]{:S(2)}) copy-start(f32[8,1536]{1,0:T(8,128)} %get-tuple-element.185) | copy-start | bytes 147460
  603.1 20.7 %copy-start.29 = (bf16[1536,64]{0,1:T(8,128)(2,1)S(1)}, bf16[1536,64]{0,1:T(8,128)(2,1)}, u32[]{:S(2)}) copy-start(bf16[1536,64]{0,1:T(8,128)(2,1)} %param.29) | copy-start | bytes 589828
  624.2 1.3 collective-permute-start.7
  (9 other events, 19.1 us)
Sparse Core Ops, SparseCore 0:
  146.1 83.6 all-gather.3
  551.4 34.9 all-reduce.1
  603.2 17.4 reduce-scatter.1
